TPU v7x, 32 devices: a whole 2x2x4 slice. The times are simulated.
32 devices in a mesh: grp: 4 (over y, x), space: 8 (over z, core).
Axes of the slice: x: 2, y: 2, z: 4, core: 2. Of those that a mesh axis runs over, the one named last changes fastest.
Arguments:
- features: bfloat16 [4, 128, 128, 128], P('grp', 'space'), may hold values from -6 to 6
- weights: bfloat16 [27, 128, 128], replicated, may hold values from -0.109375 to 0.109375
- cotangent: bfloat16 [4, 128, 128, 128], P('grp', 'space'), may hold values from -6 to 6
- kernel_map: int32 [4, 128, 27], P('grp', 'space'), may hold values from -1 to 127, as said below
- counts: int32 [4, 8], P('grp', 'space'), may hold values from 4 to 16
Outputs:
- output: bfloat16 [4, 128, 128, 128], P('grp', 'space')
- input_grad: bfloat16 [4, 128, 128, 128], P('grp', 'space')
- weight_grad: float32 [3456, 128], P('space')
Inputs may be any that keep to these rules, and one draw needn't show every extreme that they name: `kernel_map`: the centre offset k = 27 div 2 maps every block to itself. Otherwise an entry for an output block b on slab d = b div 16 is -1 or lies in [d * 16 - 4, (d + 1) * 16 + 4) within the sample. The live blocks of a device are its first counts slots.
All inputs are finite; a program needn't handle non-finite values.
Results may differ from a plain program's by a relative error of at most 0.005.
Values may be sent and summed in bfloat16 or wider, within the bound.
A program may use at most 64 MiB of HBM per device.

v0:
```python
import jax
import jax.numpy as jnp
from jax import lax
from jax.sharding import PartitionSpec as P

K = 27
H = 4


def extended_2(block, sides, width):
    for axis, dim in sides:
        count = lax.axis_size(axis)
        forward = [(i, i + 1) for i in range(count - 1)]
        backward = [(target, source) for source, target in forward]
        low = lax.ppermute(
            lax.slice_in_dim(block, block.shape[dim] - width, None, axis=dim), axis, forward
        )
        high = lax.ppermute(lax.slice_in_dim(block, 0, width, axis=dim), axis, backward)
        block = jnp.concatenate([low, block, high], axis=dim)
    return block


def passed_along(block, axis, distance):
    devices = range(lax.axis_size(axis))
    route = [(i - distance, i) for i in devices if i - distance in devices]
    return lax.ppermute(block, axis, route)


def per_device(features, weights, cotangent, kernel_map, counts):
    voxels = features[0]
    slots = voxels.shape[0]
    device = lax.axis_index("space")
    live_mask = (jnp.arange(slots) < counts[0, 0]).astype(jnp.bfloat16)[:, None, None]
    live_float = live_mask.astype(jnp.float32)
    masked = voxels * live_mask
    grad_out = cotangent[0] * live_mask
    extended = extended_2(masked, (("space", 0),), H)
    block_map = kernel_map[0]
    first_block = device * slots - H
    present = (block_map >= 0).astype(jnp.bfloat16)
    local_index = jnp.where(block_map >= 0, block_map - first_block, 0)
    channels_in = voxels.shape[2]
    channels_out = weights.shape[2]

    def step(offset, carry):
        total, grad_in, wgrad = carry
        column = lax.dynamic_index_in_dim(local_index, offset, 1, keepdims=False)
        present_k = lax.dynamic_index_in_dim(present, offset, 1, keepdims=False)[:, None, None]
        gathered = jnp.take(extended, column, axis=0) * present_k
        kernel = lax.dynamic_index_in_dim(weights, offset, 0, keepdims=False)
        total = total + jnp.einsum(
            "brc,co->bro", gathered, kernel, preferred_element_type=jnp.float32
        )
        term = jnp.einsum("bro,co->brc", grad_out, kernel, preferred_element_type=jnp.float32)
        grad_in = grad_in.at[column].add(term * present_k.astype(jnp.float32))
        piece = jnp.einsum("brc,bro->co", gathered, grad_out, preferred_element_type=jnp.float32)
        wgrad = lax.dynamic_update_index_in_dim(wgrad, piece, offset, 0)
        return (total, grad_in, wgrad)

    start = (
        jnp.zeros((slots, voxels.shape[1], channels_out), jnp.float32),
        jnp.zeros((slots + 2 * H, voxels.shape[1], channels_in), jnp.float32),
        jnp.zeros((K, channels_in, channels_out), jnp.float32),
    )
    total, grad_in, wgrad = lax.fori_loop(0, K, step, start)
    output = (total * live_float).astype(jnp.bfloat16)
    lower_rim = grad_in[:H]
    upper_rim = grad_in[slots + H :]
    own_grad = grad_in[H : slots + H]
    from_above = passed_along(lower_rim.astype(jnp.bfloat16), "space", -1).astype(lower_rim.dtype)
    from_below = passed_along(upper_rim.astype(jnp.bfloat16), "space", 1).astype(upper_rim.dtype)
    own_grad = own_grad.at[:H].add(from_below)
    own_grad = own_grad.at[slots - H :].add(from_above)
    input_grad = (own_grad * live_float).astype(jnp.bfloat16)
    weight_rows = wgrad.reshape(K * channels_in, channels_out)
    summed = lax.psum(weight_rows, ("grp", "space"))
    row_count = weight_rows.shape[0] // lax.axis_size("space")
    own_rows = lax.dynamic_slice_in_dim(summed, device * row_count, row_count, 0)
    return (output[None], input_grad[None], own_rows)


def solution(mesh):
    in_specs = (
        P("grp", "space", None, None),
        P(),
        P("grp", "space", None, None),
        P("grp", "space", None),
        P("grp", "space"),
    )
    out_specs = (P("grp", "space", None, None), P("grp", "space", None, None), P("space", None))
    return jax.shard_map(
        per_device, mesh=mesh, in_specs=in_specs, out_specs=out_specs, check_vma=False
    )
```

profile of v0, /device:TPU:0, one launch (start us, length us, event | category | flops | bytes accessed | tf_op | source)
XLA Modules:
  0.0 446.6 jit_solution(6604111132095993957)
XLA Ops:
  13.1 4.0 collective-permute-done.1
  19.4 278.4 %while.20 = (s32[]{:T(128)}, f32[16,128,128]{2,1,0:T(8,128)}, f32[24,128,128]{2,1,0:T(8,128)}, f32[27,128,128]{2,1,0:T(8,128)}, s32[16,27]{0,1:T(8,128)S(1)}, /*...) while((s32[]{:T(128)}, f32[16,128,128]{2,1,0:T(8,128)}, ...), condition=%wide.region_2.3_spmd.clone, body=%wide.region_0.2_spmd.clone.sunk | while | flops 203424880 | bytes 11670275 | solution.py:65
  24.7 3.5 scatter_fusion
  35.2 3.4 scatter_fusion
  45.6 3.3 scatter_fusion
  51.9 2.6 convolution_add_fusion.2
  55.9 3.4 scatter_fusion
  66.3 3.3 scatter_fusion
  76.6 3.3 scatter_fusion
  86.9 3.3 scatter_fusion
  97.1 3.4 scatter_fusion
  107.5 3.3 scatter_fusion
  117.8 3.3 scatter_fusion
  128.1 3.3 scatter_fusion
  138.3 3.4 scatter_fusion
  148.7 3.3 scatter_fusion
  158.9 3.4 scatter_fusion
  169.3 3.3 scatter_fusion
  179.6 3.4 scatter_fusion
  189.9 3.4 scatter_fusion
  200.3 3.4 scatter_fusion
  210.6 3.4 scatter_fusion
  220.9 3.4 scatter_fusion
  231.2 3.4 scatter_fusion
  241.6 3.3 scatter_fusion
  251.9 3.4 scatter_fusion
  262.3 3.3 scatter_fusion
  272.6 3.4 scatter_fusion
  282.9 3.3 scatter_fusion
  293.2 3.4 scatter_fusion
  299.4 6.2 %collective-permute-start.2 = (bf16[4,128,128]{2,1,0:T(8,128)(2,1)S(1)}, bf16[4,128,128]{2,1,0:T(8,128)(2,1)S(1)}, u32[]{:S(2)}, u32[]{:S(2)}) collective-permute-start(bf16[4,128,128]{2,1,0:T(8,128)(2,1)S(1)} %get-tuple-element.239), channel_id=1, source_target_pairs={{0,1},{1,2},{2,3},{3,4},{4,5},{5,6},{6,7},{8,9},{9,10},{10,11},{11... | collective-permute-start | bytes 393224 | tf_op jit(solution)/shard_map/ppermute | solution.py:26
  311.6 126.6 %all-reduce.2.cloned.1.call-done = f32[3456,128]{1,0:T(8,128)} async-done(((f32[3456,128]{1,0:T(8,128)}), f32[3456,128]{1,0:T(8,128)}) %all-reduce.2.cloned.1.call-update) | async-done | bytes 1769488 | tf_op jit(solution)/shard_map/psum | solution.py:76
  (245 shorter events, 200.7 us)
Async XLA Ops:
  7.2 5.8 %copy-start.1 = (s32[1,16,27]{2,1,0:T(8,128)S(1)}, s32[1,16,27]{2,1,0:T(8,128)}, u32[]{:S(2)}) copy-start(s32[1,16,27]{2,1,0:T(8,128)} %param.14) | copy-start | bytes 5188
  7.2 431.0 %all-reduce.2.cloned.1.call-start = ((), (), s32[]{:S(2)}) async-start(), calls=%async_computation | async-start | bytes 3538944 | tf_op jit(solution)/shard_map/psum | solution.py:76
  9.2 3.8 collective-permute-start
  11.7 5.4 %collective-permute-start.1 = (bf16[4,128,128]{2,1,0:T(8,128)(2,1)S(1)}, bf16[4,128,128]{2,1,0:T(8,128)(2,1)S(1)}, u32[]{:S(2)}, u32[]{:S(2)}) collective-permute-start(bf16[4,128,128]{2,1,0:T(8,128)(2,1)S(1)} %get-tuple-element.241), channel_id=1, source_target_pairs={{1,0},{2,1},{3,2},{4,3},{5,4},{6,5},{7,6},{9,8},{10,9},{11,10},{12... | collective-permute-start | bytes 393224 | tf_op jit(solution)/shard_map/ppermute | solution.py:18
  297.7 7.9 %copy-start = (f32[24,128,128]{2,1,0:T(8,128)S(1)}, f32[24,128,128]{2,1,0:T(8,128)}, u32[]{:S(2)}) copy-start(f32[24,128,128]{2,1,0:T(8,128)} %get-tuple-element.184) | copy-start | bytes 4718596
  299.4 7.6 %collective-permute-start.2 = (bf16[4,128,128]{2,1,0:T(8,128)(2,1)S(1)}, bf16[4,128,128]{2,1,0:T(8,128)(2,1)S(1)}, u32[]{:S(2)}, u32[]{:S(2)}) collective-permute-start(bf16[4,128,128]{2,1,0:T(8,128)(2,1)S(1)} %get-tuple-element.239), channel_id=1, source_target_pairs={{0,1},{1,2},{2,3},{3,4},{4,5},{5,6},{6,7},{8,9},{9,10},{10,11},{11... | collective-permute-start | bytes 393224 | tf_op jit(solution)/shard_map/ppermute | solution.py:26
  305.8 3.2 collective-permute-start.3
Sparse Core Ops, SparseCore 0:
  305.8 132.3 all-reduce.1
where the time goes:
time: 453 us; the launch traced here: 447 us
  waiting for transfers between devices  132 us (29%)
  matrix products  129 us (28%)
  other arithmetic  98.1 us (22%)
  local copies, waits for them, and re-layouts  60.2 us (13%)
  between operations  14.8 us (3%)
  starting transfers between devices  11.2 us (2%)
    psum x1, waiting for transfers between devices, per_device(): summed = lax.psum(weight_rows, ('grp', 'space'))  127 us
    scatter-add x27, other arithmetic, step(): grad_in = grad_in.at[column].add(term * present_k.astype(jnp.float32))  90.8 us
    dot_general x27, matrix products, step(): jnp.einsum('brc,co->bro', gathered, kernel, preferred_element_type=jnp.fl...  70 us
    gather x27, local copies, waits for them, and re-layouts, step(): gathered = jnp.take(extended, column, axis=0) * present_k  48.1 us
    dot_general x27, matrix products, step(): jnp.einsum('brc,bro->co', gathered, grad_out, preferred_element_type=jnp....  30.5 us
    dot_general x27, matrix products, step(): jnp.einsum('bro,co->brc', grad_out, kernel, preferred_element_type=jnp.fl...  28.4 us
  transfers between devices with their start and end apart: 5, of which 3 were waited for; matrix products, arithmetic and copies ran while one was open for 1% of the time, Pallas kernels for 0%

commit v1 on v0

--- a/solution.py
+++ b/solution.py
@@ -73,7 +73,7 @@
     own_grad = own_grad.at[slots - H :].add(from_above)
     input_grad = (own_grad * live_float).astype(jnp.bfloat16)
     weight_rows = wgrad.reshape(K * channels_in, channels_out)
-    summed = lax.psum(weight_rows, ("grp", "space"))
+    summed = lax.psum(lax.psum(weight_rows, "grp"), "space")
     row_count = weight_rows.shape[0] // lax.axis_size("space")
     own_rows = lax.dynamic_slice_in_dim(summed, device * row_count, row_count, 0)
     return (output[None], input_grad[None], own_rows)

time: 453 us -> 446 us (0.985)
  waiting for transfers between devices: 132 us -> 126 us
    psum x1 -> x2, waiting for transfers between devices: 127 us -> 120 us  [per_device(): summed = lax.psum(lax.psum(weight_rows, 'grp'), 'space')]
  transfers between devices with their start and end apart: 5 -> 6, of which waited for: 3 -> 4; matrix products, arithmetic and copies ran while one was open for 1% -> 1% of each run, Pallas kernels for 0% -> 0%
where the time goes in v1:
time: 446 us; the launch traced here: 440 us
  matrix products  129 us (29%)
  waiting for transfers between devices  126 us (28%)
  other arithmetic  96.6 us (22%)
  local copies, waits for them, and re-layouts  61.5 us (14%)
  between operations  14.8 us (3%)
  starting transfers between devices  11.2 us (3%)
    psum x2, waiting for transfers between devices, per_device(): summed = lax.psum(lax.psum(weight_rows, 'grp'), 'space')  120 us
    scatter-add x27, other arithmetic, step(): grad_in = grad_in.at[column].add(term * present_k.astype(jnp.float32))  90.8 us
    dot_general x27, matrix products, step(): jnp.einsum('brc,co->bro', gathered, kernel, preferred_element_type=jnp.fl...  70 us
    gather x27, local copies, waits for them, and re-layouts, step(): gathered = jnp.take(extended, column, axis=0) * present_k  48.1 us
    dot_general x27, matrix products, step(): jnp.einsum('brc,bro->co', gathered, grad_out, preferred_element_type=jnp....  30.5 us
    dot_general x27, matrix products, step(): jnp.einsum('bro,co->brc', grad_out, kernel, preferred_element_type=jnp.fl...  28.4 us
    mul x27, local copies, waits for them, and re-layouts, step(): grad_in = grad_in.at[column].add(term * present_k.astype(jnp.float32))  8.94 us
  transfers between devices with their start and end apart: 6, of which 4 were waited for; matrix products, arithmetic and copies ran while one was open for 1% of the time, Pallas kernels for 0%

profile of v1, /device:TPU:0, one launch (start us, length us, event | category | flops | bytes accessed | tf_op | source)
XLA Modules:
  0.0 439.6 jit_solution(15036566858600868694)
XLA Ops:
  13.1 4.0 collective-permute-done.1
  19.4 278.4 %while.20 = (s32[]{:T(128)}, f32[16,128,128]{2,1,0:T(8,128)}, f32[24,128,128]{2,1,0:T(8,128)}, f32[27,128,128]{2,1,0:T(8,128)}, s32[16,27]{0,1:T(8,128)S(1)}, /*...) while((s32[]{:T(128)}, f32[16,128,128]{2,1,0:T(8,128)}, ...), condition=%wide.region_2.3_spmd.clone, body=%wide.region_0.2_spmd.clone.sunk | while | flops 203424880 | bytes 11670275 | solution.py:65
  24.7 3.5 scatter_fusion
  35.2 3.4 scatter_fusion
  45.6 3.3 scatter_fusion
  55.9 3.4 scatter_fusion
  66.3 3.3 scatter_fusion
  76.6 3.3 scatter_fusion
  86.9 3.3 scatter_fusion
  97.1 3.4 scatter_fusion
  107.5 3.3 scatter_fusion
  117.8 3.3 scatter_fusion
  128.1 3.3 scatter_fusion
  138.3 3.4 scatter_fusion
  148.7 3.3 scatter_fusion
  158.9 3.4 scatter_fusion
  169.3 3.3 scatter_fusion
  179.6 3.4 scatter_fusion
  189.9 3.4 scatter_fusion
  200.3 3.4 scatter_fusion
  210.6 3.4 scatter_fusion
  220.9 3.4 scatter_fusion
  231.2 3.4 scatter_fusion
  241.6 3.3 scatter_fusion
  251.9 3.4 scatter_fusion
  262.3 3.3 scatter_fusion
  272.6 3.4 scatter_fusion
  282.9 3.3 scatter_fusion
  293.2 3.4 scatter_fusion
  299.3 6.2 %collective-permute-start.2 = (bf16[4,128,128]{2,1,0:T(8,128)(2,1)S(1)}, bf16[4,128,128]{2,1,0:T(8,128)(2,1)S(1)}, u32[]{:S(2)}, u32[]{:S(2)}) collective-permute-start(bf16[4,128,128]{2,1,0:T(8,128)(2,1)S(1)} %get-tuple-element.239), channel_id=1, source_target_pairs={{0,1},{1,2},{2,3},{3,4},{4,5},{5,6},{6,7},{8,9},{9,10},{10,11},{11... | collective-permute-start | bytes 393224 | tf_op jit(solution)/shard_map/ppermute | solution.py:26
  305.5 60.0 %all-reduce.3.cloned.1.call-done = f32[3456,128]{1,0:T(8,128)} async-done(((f32[3456,128]{1,0:T(8,128)}), f32[3456,128]{1,0:T(8,128)}) %all-reduce.3.cloned.1.call-update) | async-done | bytes 1769488 | tf_op jit(solution)/shard_map/psum | solution.py:76
  371.4 59.8 %all-reduce.5.cloned.1.call-done = f32[3456,128]{1,0:T(8,128)} async-done(((f32[3456,128]{1,0:T(8,128)}), f32[3456,128]{1,0:T(8,128)}) %all-reduce.5.cloned.1.call-update) | async-done | bytes 1769488 | tf_op jit(solution)/shard_map/psum | solution.py:76
  (248 shorter events, 203.2 us)
Async XLA Ops:
  7.2 5.8 %copy-start.1 = (s32[1,16,27]{2,1,0:T(8,128)S(1)}, s32[1,16,27]{2,1,0:T(8,128)}, u32[]{:S(2)}) copy-start(s32[1,16,27]{2,1,0:T(8,128)} %param.14) | copy-start | bytes 5188
  7.2 358.3 %all-reduce.3.cloned.1.call-start = ((), (), s32[]{:S(2)}) async-start(), calls=%async_computation | async-start | bytes 3538944 | tf_op jit(solution)/shard_map/psum | solution.py:76
  9.2 3.8 collective-permute-start
  11.7 5.4 %collective-permute-start.1 = (bf16[4,128,128]{2,1,0:T(8,128)(2,1)S(1)}, bf16[4,128,128]{2,1,0:T(8,128)(2,1)S(1)}, u32[]{:S(2)}, u32[]{:S(2)}) collective-permute-start(bf16[4,128,128]{2,1,0:T(8,128)(2,1)S(1)} %get-tuple-element.241), channel_id=1, source_target_pairs={{1,0},{2,1},{3,2},{4,3},{5,4},{6,5},{7,6},{9,8},{10,9},{11,10},{12... | collective-permute-start | bytes 393224 | tf_op jit(solution)/shard_map/ppermute | solution.py:18
  297.7 1.4 copy-start
  297.8 133.4 %all-reduce.5.cloned.1.call-start = ((), (), s32[]{:S(2)}) async-start(), calls=%async_computation.1 | async-start | bytes 3538944 | tf_op jit(solution)/shard_map/psum | solution.py:76
  299.3 67.6 %collective-permute-start.2 = (bf16[4,128,128]{2,1,0:T(8,128)(2,1)S(1)}, bf16[4,128,128]{2,1,0:T(8,128)(2,1)S(1)}, u32[]{:S(2)}, u32[]{:S(2)}) collective-permute-start(bf16[4,128,128]{2,1,0:T(8,128)(2,1)S(1)} %get-tuple-element.239), channel_id=1, source_target_pairs={{0,1},{1,2},{2,3},{3,4},{4,5},{5,6},{6,7},{8,9},{9,10},{10,11},{11... | collective-permute-start | bytes 393224 | tf_op jit(solution)/shard_map/ppermute | solution.py:26
  365.6 3.2 collective-permute-start.3
Sparse Core Ops, SparseCore 0:
  297.9 67.5 all-reduce.2
  367.8 63.2 all-reduce.4
